TPU v7x, 32 devices: a whole 2x2x4 slice. The times are simulated.
32 devices in a mesh: fsdp: 16 (over z, y, core), sp: 2 (over x).
Axes of the slice: x: 2, y: 2, z: 4, core: 2. Of those that a mesh axis runs over, the one named last changes fastest.
Arguments:
- latents: bfloat16 [32, 256, 768], P('fsdp', 'sp'), may hold values from -6 to 6
- condition: bfloat16 [32, 768], P('fsdp'), may hold values from -6 to 6
- cotangent: bfloat16 [32, 256, 768], P('fsdp', 'sp'), may hold values from -6 to 6
- w_ada: bfloat16 [768, 4608], P('fsdp'), may hold values from -0.21875 to 0.21875
- b_ada: bfloat16 [4608], P('fsdp'), may hold values from -3 to 3
- w_qkv: bfloat16 [768, 2304], P('fsdp'), may hold values from -0.21875 to 0.21875
- b_query: bfloat16 [768], P('fsdp'), may hold values from -3 to 3
- b_value: bfloat16 [768], P('fsdp'), may hold values from -3 to 3
- w_out: bfloat16 [768, 768], P('fsdp'), may hold values from -0.875 to 0.875
- b_out: bfloat16 [768], P('fsdp'), may hold values from -3 to 3
- w_up: bfloat16 [768, 3072], P('fsdp'), may hold values from -0.21875 to 0.21875
- b_up: bfloat16 [3072], P('fsdp'), may hold values from -3 to 3
- w_down: bfloat16 [3072, 768], P('fsdp'), may hold values from -0.109375 to 0.109375
- b_down: bfloat16 [768], P('fsdp'), may hold values from -3 to 3
Outputs:
- output: bfloat16 [32, 256, 768], P('fsdp', 'sp')
- grad_latents: float32 [32, 256, 768], P('fsdp', 'sp')
- grad_condition: float32 [32, 768], P('fsdp')
- grad_w_ada: float32 [768, 4608], P(('fsdp', 'sp'))
- grad_b_ada: float32 [4608], P(('fsdp', 'sp'))
- grad_w_qkv: float32 [768, 2304], P(('fsdp', 'sp'))
- grad_b_query: float32 [768], P(('fsdp', 'sp'))
- grad_b_value: float32 [768], P(('fsdp', 'sp'))
- grad_w_out: float32 [768, 768], P(('fsdp', 'sp'))
- grad_b_out: float32 [768], P(('fsdp', 'sp'))
- grad_w_up: float32 [768, 3072], P(('fsdp', 'sp'))
- grad_b_up: float32 [3072], P(('fsdp', 'sp'))
- grad_w_down: float32 [3072, 768], P(('fsdp', 'sp'))
- grad_b_down: float32 [768], P(('fsdp', 'sp'))
All inputs are finite; a program needn't handle non-finite values.
Results may differ from a plain program's by a relative error of at most 0.015.
The roundings to bfloat16 on the way count: a program that leaves them out, or rounds other values in their place, can miss the bound.
Values may be sent and summed in bfloat16 or wider, within the bound.
A program may use at most 256 MiB of HBM per device.

v0:
```python
import jax
import jax.numpy as jnp
from jax import lax
from jax.sharding import PartitionSpec as P

D = 768
H = 12
HD = 64
eps = 1e-06


def normalize(values):
    centered = values - jnp.mean(values, axis=-1, keepdims=True)
    inverse = lax.rsqrt(jnp.mean(centered * centered, axis=-1, keepdims=True) + eps)
    return (centered * inverse, inverse)


def norm_back(grad_in, normed, inverse):
    return inverse * (
        grad_in
        - jnp.mean(grad_in, axis=-1, keepdims=True)
        - normed * jnp.mean(grad_in * normed, axis=-1, keepdims=True)
    )


def gelu_tanh(values):
    return jax.nn.gelu(values, approximate=True)


def silu_back(values, grad_out):
    return jax.vjp(jax.nn.silu, values)[1](grad_out)[0]


def gelu_back(values, grad_out):
    return jax.vjp(gelu_tanh, values)[1](grad_out)[0]


LANES = 2048


def reduce_rows(grad):
    return lax.psum_scatter(
        grad.astype(jnp.bfloat16), ("fsdp", "sp"), scatter_dimension=0, tiled=True
    ).astype(jnp.float32)


def body(
    latents,
    condition,
    cotangent,
    w_ada,
    b_ada,
    w_qkv,
    b_query,
    b_value,
    w_out,
    b_out,
    w_up,
    b_up,
    w_down,
    b_down,
):
    f32 = jnp.float32
    bf16 = jnp.bfloat16
    fsdp_count = lax.axis_size("fsdp")
    sp_count = lax.axis_size("sp")
    owners = fsdp_count * sp_count
    fsdp_index = lax.axis_index("fsdp")
    sp_index = lax.axis_index("sp")
    owner_index = fsdp_index * sp_count + sp_index
    pair_latents = latents.shape[0]
    own_latents = pair_latents // sp_count
    latent_total = pair_latents * fsdp_count
    tokens_all = latents.shape[1] * sp_count
    scale_factor = HD ** (-0.5)
    small = [condition.reshape(-1), b_ada, b_query, b_value, b_out, b_up, b_down]
    width = sum((part.size for part in small))
    padded = -(-width // LANES) * LANES
    small.append(jnp.zeros((padded - width,), bf16))
    small_all = lax.all_gather(
        jnp.concatenate(small).reshape(1, padded // 128, 128), "fsdp", axis=0, tiled=True
    ).reshape(fsdp_count, padded)
    pieces = []
    start = 0
    for part in small[:-1]:
        pieces.append(small_all[:, start : start + part.size].reshape(-1))
        start = start + part.size
    cond_all, ada_bias, query_bias, value_bias, out_bias, up_bias, down_bias = pieces
    cond_all = cond_all.reshape(latent_total, D).astype(f32)
    silu_all = jax.nn.silu(cond_all)
    inputs = lax.all_to_all(latents, "sp", split_axis=0, concat_axis=1, tiled=True).astype(f32)
    grad_out = lax.all_to_all(cotangent, "sp", split_axis=0, concat_axis=1, tiled=True).astype(f32)
    ada_rows = w_ada.shape[0]
    silu_mine = lax.dynamic_index_in_dim(
        silu_all.astype(bf16).reshape(fsdp_count, sp_count, own_latents, D), sp_index, 1, False
    )
    silu_mine = lax.dynamic_index_in_dim(
        silu_mine.reshape(fsdp_count * own_latents, fsdp_count, ada_rows), fsdp_index, 1, False
    )
    mod_part = jnp.dot(silu_mine, w_ada, preferred_element_type=f32)
    mod_part = lax.all_to_all(
        mod_part.reshape(fsdp_count, own_latents * 6 * D),
        "fsdp",
        split_axis=0,
        concat_axis=0,
        tiled=True,
    )
    modulate = jnp.sum(mod_part, axis=0).reshape(own_latents, 6 * D) + ada_bias.astype(f32)
    mod_parts = modulate.reshape(own_latents, 6, 1, D)
    shift_one, scale_one, gate_one = (mod_parts[:, 0], mod_parts[:, 1], mod_parts[:, 2])
    shift_two, scale_two, gate_two = (mod_parts[:, 3], mod_parts[:, 4], mod_parts[:, 5])
    qkv_full = lax.all_gather(w_qkv, "fsdp", axis=0, tiled=True)
    out_full = lax.all_gather(w_out, "fsdp", axis=0, tiled=True)
    up_full = lax.all_gather(w_up, "fsdp", axis=0, tiled=True)
    down_full = lax.all_gather(w_down, "fsdp", axis=0, tiled=True)
    normed_one, inverse_one = normalize(inputs)
    attn_in = (normed_one * (1.0 + scale_one) + shift_one).astype(bf16)
    qkv_bias = jnp.concatenate([query_bias, jnp.zeros_like(query_bias), value_bias]).astype(f32)
    projected = (
        jnp.einsum("btd,de->bte", attn_in, qkv_full, preferred_element_type=f32) + qkv_bias
    ).astype(bf16)
    heads = projected.reshape(own_latents, tokens_all, 3, H, HD).transpose(2, 0, 3, 1, 4)
    queries, key_heads, value_heads = (heads[0], heads[1], heads[2])
    scores = (
        jnp.einsum("bhqd,bhkd->bhqk", queries, key_heads, preferred_element_type=f32) * scale_factor
    )
    log_total = jnp.log(jnp.sum(jnp.exp(scores), axis=-1, keepdims=True))
    soft_float = jnp.exp(scores - log_total)
    soft_half = soft_float.astype(bf16)
    mixed = jnp.einsum(
        "bhqk,bhkd->bhqd", soft_half, value_heads, preferred_element_type=f32
    ).astype(bf16)
    mixed_tokens = mixed.transpose(0, 2, 1, 3).reshape(own_latents, tokens_all, D)
    attn_proj = jnp.einsum(
        "btd,de->bte", mixed_tokens, out_full, preferred_element_type=f32
    ) + out_bias.astype(f32)
    residual = inputs + gate_one * attn_proj
    normed_two, inverse_two = normalize(residual)
    mlp_in = (normed_two * (1.0 + scale_two) + shift_two).astype(bf16)
    up_value = jnp.einsum(
        "btd,df->btf", mlp_in, up_full, preferred_element_type=f32
    ) + up_bias.astype(f32)
    activated = gelu_tanh(up_value).astype(bf16)
    down_value = jnp.einsum(
        "btf,fd->btd", activated, down_full, preferred_element_type=f32
    ) + down_bias.astype(f32)
    output = (residual + gate_two * down_value).astype(bf16)
    output = lax.all_to_all(output, "sp", split_axis=1, concat_axis=0, tiled=True)
    grad_gate_two = jnp.sum(grad_out * down_value, axis=1)
    grad_down = (grad_out * gate_two).astype(bf16)
    gw_down = jnp.einsum("btf,btd->fd", activated, grad_down, preferred_element_type=f32)
    own_down = reduce_rows(gw_down)
    gb_down = jnp.sum(grad_down.astype(f32), axis=(0, 1))
    grad_act = jnp.einsum("btd,fd->btf", grad_down, down_full, preferred_element_type=f32)
    grad_up = gelu_back(up_value, grad_act).astype(bf16)
    gw_up = jnp.einsum("btd,btf->df", mlp_in, grad_up, preferred_element_type=f32)
    own_up = reduce_rows(gw_up)
    gb_up = jnp.sum(grad_up.astype(f32), axis=(0, 1))
    grad_mlp = jnp.einsum("btf,df->btd", grad_up, up_full, preferred_element_type=f32)
    grad_scale_two = jnp.sum(grad_mlp * normed_two, axis=1)
    grad_shift_two = jnp.sum(grad_mlp, axis=1)
    grad_resid = grad_out + norm_back(grad_mlp * (1.0 + scale_two), normed_two, inverse_two)
    grad_gate_one = jnp.sum(grad_resid * attn_proj, axis=1)
    grad_proj = (grad_resid * gate_one).astype(bf16)
    gw_out = jnp.einsum("btd,bte->de", mixed_tokens, grad_proj, preferred_element_type=f32)
    own_out = reduce_rows(gw_out)
    gb_out = jnp.sum(grad_proj.astype(f32), axis=(0, 1))
    grad_mixed = jnp.einsum("bte,de->btd", grad_proj, out_full, preferred_element_type=f32).astype(
        bf16
    )
    grad_heads = grad_mixed.reshape(own_latents, tokens_all, H, HD).transpose(0, 2, 1, 3)
    grad_soft = jnp.einsum("bhqd,bhkd->bhqk", grad_heads, value_heads, preferred_element_type=f32)
    delta_sum = jnp.sum(soft_float * grad_soft, axis=-1, keepdims=True)
    grad_scores = (soft_float * (grad_soft - delta_sum)).astype(bf16)
    grad_queries = (
        jnp.einsum("bhqk,bhkd->bhqd", grad_scores, key_heads, preferred_element_type=f32)
        * scale_factor
    ).astype(bf16)
    grad_keys = (
        jnp.einsum("bhqk,bhqd->bhkd", grad_scores, queries, preferred_element_type=f32)
        * scale_factor
    ).astype(bf16)
    grad_values = jnp.einsum(
        "bhqk,bhqd->bhkd", soft_half, grad_heads, preferred_element_type=f32
    ).astype(bf16)
    grad_tokens = (
        jnp.stack([grad_queries, grad_keys, grad_values], axis=0)
        .transpose(1, 3, 0, 2, 4)
        .reshape(own_latents, tokens_all, 3 * D)
    )
    gw_qkv = jnp.einsum("btd,bte->de", attn_in, grad_tokens, preferred_element_type=f32)
    own_qkv = reduce_rows(gw_qkv)
    grad_tok_float = grad_tokens.astype(f32)
    gb_query = jnp.sum(grad_tok_float[:, :, :D], axis=(0, 1))
    gb_value = jnp.sum(grad_tok_float[:, :, 2 * D :], axis=(0, 1))
    grad_attn_in = jnp.einsum("bte,de->btd", grad_tokens, qkv_full, preferred_element_type=f32)
    grad_scale_one = jnp.sum(grad_attn_in * normed_one, axis=1)
    grad_shift_one = jnp.sum(grad_attn_in, axis=1)
    grad_latents = grad_resid + norm_back(grad_attn_in * (1.0 + scale_one), normed_one, inverse_one)
    grad_latents = lax.all_to_all(grad_latents, "sp", split_axis=1, concat_axis=0, tiled=True)
    grad_small = [
        grad_shift_one.reshape(-1),
        grad_scale_one.reshape(-1),
        grad_gate_one.reshape(-1),
        grad_shift_two.reshape(-1),
        grad_scale_two.reshape(-1),
        grad_gate_two.reshape(-1),
        gb_query,
        gb_value,
        gb_out,
        gb_up,
        gb_down,
    ]
    grad_small_all = lax.all_gather(jnp.concatenate(grad_small), ("fsdp", "sp"), axis=0)
    mod_width = 6 * own_latents * D
    grad_mod = (
        grad_small_all[:, :mod_width]
        .reshape(owners, 6, own_latents, D)
        .transpose(0, 2, 1, 3)
        .reshape(latent_total, 6 * D)
    )
    bias_sums = jnp.sum(grad_small_all[:, mod_width:], axis=0)
    own_bias = []
    start = 0
    for part in grad_small[6:]:
        piece = bias_sums[start : start + part.size].reshape(owners, -1)
        own_bias.append(lax.dynamic_index_in_dim(piece, owner_index, 0, False))
        start = start + part.size
    own_gb_query, own_gb_value, own_gb_out, own_gb_up, own_gb_down = own_bias
    silu_rows = lax.dynamic_index_in_dim(
        silu_all.reshape(latent_total, owners, D // owners), owner_index, 1, False
    )
    own_ada = jnp.dot(silu_rows.T, grad_mod, precision=lax.Precision.HIGHEST)
    own_gb_ada = lax.dynamic_index_in_dim(
        jnp.sum(grad_mod, axis=0).reshape(owners, -1), owner_index, 0, False
    )
    grad_silu = jnp.dot(grad_mod.astype(bf16), w_ada.T, preferred_element_type=f32)
    grad_silu = lax.all_to_all(
        grad_silu.reshape(fsdp_count, pair_latents * ada_rows),
        "fsdp",
        split_axis=0,
        concat_axis=0,
        tiled=True,
    )
    grad_silu = (
        grad_silu.reshape(fsdp_count, pair_latents, ada_rows)
        .transpose(1, 0, 2)
        .reshape(pair_latents, D)
    )
    grad_condition = silu_back(condition.astype(f32), grad_silu)
    return (
        output,
        grad_latents,
        grad_condition,
        own_ada,
        own_gb_ada,
        own_qkv,
        own_gb_query,
        own_gb_value,
        own_out,
        own_gb_out,
        own_up,
        own_gb_up,
        own_down,
        own_gb_down,
    )


def solution(mesh):
    in_specs = (
        P("fsdp", "sp", None),
        P("fsdp", None),
        P("fsdp", "sp", None),
        P("fsdp", None),
        P("fsdp"),
        P("fsdp", None),
        P("fsdp"),
        P("fsdp"),
        P("fsdp", None),
        P("fsdp"),
        P("fsdp", None),
        P("fsdp"),
        P("fsdp", None),
        P("fsdp"),
    )
    out_specs = (
        P("fsdp", "sp", None),
        P("fsdp", "sp", None),
        P("fsdp", None),
        P(("fsdp", "sp"), None),
        P(("fsdp", "sp")),
        P(("fsdp", "sp"), None),
        P(("fsdp", "sp")),
        P(("fsdp", "sp")),
        P(("fsdp", "sp"), None),
        P(("fsdp", "sp")),
        P(("fsdp", "sp"), None),
        P(("fsdp", "sp")),
        P(("fsdp", "sp"), None),
        P(("fsdp", "sp")),
    )
    return jax.shard_map(body, mesh=mesh, in_specs=in_specs, out_specs=out_specs, check_vma=False)
```

profile of v0, /device:TPU:0, one launch (start us, length us, event | category | flops | bytes accessed | tf_op | source)
XLA Modules:
  0.0 743.5 jit_solution(2040132775007080298)
XLA Ops:
  8.0 0.7 all-gather.10.cloned.1.call-update
  10.0 4.2 all-to-all-start
  14.2 0.7 reshape.743
  14.9 4.1 concatenate.17
  19.1 22.7 %all_gather.21 = bf16[16,32,128]{2,1,0:T(8,128)(2,1)S(1)} all-gather(bf16[1,32,128]{2,1,0:T(8,128)(2,1)S(1)} %bitcast.185), channel_id=1, replica_groups=mesh['fsdp'=16,'sp'=2] {'fsdp'}, dimensions={0}, use_global_device_ids=true | all-gather | bytes 139264 | tf_op jit(solution)/shard_map/all_gather | solution.py:80
  42.4 1.0 copy.61
  43.7 3.5 all-to-all-start.1
  48.0 13.6 %all-to-all-done.1 = f32[16,1,4608]{2,1,0:T(1,128)S(1)} async-done(((f32[16,1,4608]{2,1,0:T(1,128)}), f32[16,1,4608]{2,1,0:T(1,128)S(1)}, u32[]{:S(2)}, u32[]{:S(2)}) %all-to-all-start.1) | async-done | bytes 294944 | tf_op jit(solution)/shard_map/all_to_all | solution.py:101
  61.7 3.8 all-to-all-start.3
  65.8 6.4 all-to-all-done.3
  72.3 0.8 fusion.21
  73.4 4.2 fusion.1
  77.6 1.6 copy.62
  79.1 2.3 fusion.55
  81.4 4.8 convolution_convert_fusion.4
  86.2 18.5 %all-gather.10.cloned.1.call-done = bf16[768,768]{1,0:T(8,128)(2,1)} async-done(((bf16[48,768]{1,0:T(8,128)(2,1)}), bf16[768,768]{1,0:T(8,128)(2,1)}) %all-gather.10.cloned.1.call-update) | async-done | bytes 1179664 | tf_op jit(solution)/shard_map/all_gather | solution.py:113
  104.6 2.8 fusion.81
  107.7 51.3 %all-gather.14.cloned.1.call-done = bf16[3072,768]{1,0:T(8,128)(2,1)} async-done(((bf16[192,768]{1,0:T(8,128)(2,1)}), bf16[3072,768]{1,0:T(8,128)(2,1)}) %all-gather.14.cloned.1.call-update) | async-done | bytes 4718608 | tf_op jit(solution)/shard_map/all_gather | solution.py:115
  159.0 5.5 fusion.83
  164.5 48.3 %all-gather.12.cloned.1.call-done = bf16[768,3072]{1,0:T(8,128)(2,1)} async-done(((bf16[48,3072]{1,0:T(8,128)(2,1)}), bf16[768,3072]{1,0:T(8,128)(2,1)}) %all-gather.12.cloned.1.call-update) | async-done | bytes 4718608 | tf_op jit(solution)/shard_map/all_gather | solution.py:114
  212.8 7.0 convert_reduce_fusion
  219.9 1.8 multiply_reduce_fusion.1
  222.2 1.7 copy-done.3
  223.9 3.2 fusion.22
  227.1 0.7 copy-done.10
  228.4 0.9 copy.66
  229.3 4.8 fusion.17
  234.7 1.3 copy-done.1
  236.0 2.9 multiply_reduce_fusion
  239.5 1.3 fusion.19
  240.8 1.2 fusion.18
  242.0 1.5 convolution_convert_fusion.3
  243.5 1.4 pad_maximum_fusion
  244.9 4.2 fusion.36
  249.0 1.6 convert.10
  250.7 3.0 multiply_reduce_fusion.2
  255.1 2.9 convolution_convert_fusion.2
  258.1 1.3 copy-done.8
  259.5 3.7 convolution_convert_fusion.1
  264.1 6.3 convolution_convert_fusion
  270.5 1.0 copy-done.13
  272.6 3.0 reduce.57
  275.6 0.8 reshape.788
  276.5 3.5 all-to-all-start.2
  279.9 1.7 copy.70
  281.6 5.5 all-to-all-done.2
  287.2 3.5 all-to-all-start.4
  291.6 0.8 copy.78
  292.4 11.1 %all-to-all-done.4 = f32[1,256,768]{2,0,1:T(1,128)S(1)} async-done(((f32[1,256,768]{2,0,1:T(1,128)}), f32[1,256,768]{2,0,1:T(1,128)S(1)}, u32[]{:S(2)}, u32[]{:S(2)}) %all-to-all-start.4) | async-done | bytes 786464 | tf_op jit(solution)/shard_map/all_to_all | solution.py:200
  303.4 0.9 copy.79
  304.4 42.0 %reduce-scatter.7.cloned.1.call-done = bf16[24,768]{1,0:T(8,128)(2,1)} async-done(((bf16[768,768]{1,0:T(8,128)(2,1)}), bf16[24,768]{1,0:T(8,128)(2,1)}) %reduce-scatter.7.cloned.1.call-update) | async-done | bytes 36880 | tf_op jit(solution)/shard_map/reduce_scatter | solution.py:42
  346.3 1.4 convert_element_type.318
  347.7 55.6 %all-gather.16.cloned.1.call-done = f32[32,1,10752]{2,1,0:T(1,128)} async-done(((f32[1,1,10752]{2,1,0:T(1,128)}), f32[32,1,10752]{2,1,0:T(1,128)}) %all-gather.16.cloned.1.call-update) | async-done | bytes 1376272 | tf_op jit(solution)/shard_map/all_gather | solution.py:214
  403.3 1.4 copy.91
  405.0 0.7 all_to_all.52
  405.7 4.6 all-to-all-start.5
  413.6 1.3 fusion.43
  415.4 1.2 all-to-all-done.5
  418.6 92.5 %reduce-scatter.5.cloned.1.call-done = bf16[24,2304]{1,0:T(8,128)(2,1)} async-done(((bf16[768,2304]{1,0:T(8,128)(2,1)}), bf16[24,2304]{1,0:T(8,128)(2,1)}) %reduce-scatter.5.cloned.1.call-update) | async-done | bytes 110608 | tf_op jit(solution)/shard_map/reduce_scatter | solution.py:42
  511.1 1.6 convert_element_type.316
  512.7 110.3 %reduce-scatter.9.cloned.1.call-done = bf16[24,3072]{1,0:T(8,128)(2,1)} async-done(((bf16[768,3072]{1,0:T(8,128)(2,1)}), bf16[24,3072]{1,0:T(8,128)(2,1)}) %reduce-scatter.9.cloned.1.call-update) | async-done | bytes 147472 | tf_op jit(solution)/shard_map/reduce_scatter | solution.py:42
  623.0 1.6 convert_element_type.320
  624.6 110.7 %reduce-scatter.11.cloned.1.call-done = bf16[96,768]{1,0:T(8,128)(2,1)} async-done(((bf16[3072,768]{1,0:T(8,128)(2,1)}), bf16[96,768]{1,0:T(8,128)(2,1)}) %reduce-scatter.11.cloned.1.call-update) | async-done | bytes 147472 | tf_op jit(solution)/shard_map/reduce_scatter | solution.py:42
  735.3 1.6 convert_element_type.322
  (131 shorter events, 17.1 us)
Async XLA Ops:
  7.2 35.0 %copy-start = (bf16[48,4608]{1,0:T(8,128)(2,1)S(1)}, bf16[48,4608]{1,0:T(8,128)(2,1)}, u32[]{:S(2)}) copy-start(bf16[48,4608]{1,0:T(8,128)(2,1)} %param.17) | copy-start | bytes 1327108
  7.2 66.2 %all-gather.8.cloned.1.call-start = ((), (), s32[]{:S(2)}) async-start(), calls=%async_computation.10 | async-start | bytes 3760128 | tf_op jit(solution)/shard_map/all_gather | solution.py:112
  7.9 96.7 %all-gather.10.cloned.1.call-start = ((), (), s32[]{:S(2)}) async-start(), calls=%async_computation.11 | async-start | bytes 1253376 | tf_op jit(solution)/shard_map/all_gather | solution.py:113
  8.7 150.3 %all-gather.14.cloned.1.call-start = ((), (), s32[]{:S(2)}) async-start(), calls=%async_computation.13 | async-start | bytes 5013504 | tf_op jit(solution)/shard_map/all_gather | solution.py:115
  9.4 203.4 %all-gather.12.cloned.1.call-start = ((), (), s32[]{:S(2)}) async-start(), calls=%async_computation.12 | async-start | bytes 5013504 | tf_op jit(solution)/shard_map/all_gather | solution.py:114
  10.0 33.7 %all-to-all-start = ((bf16[2,128,768]{2,1,0:T(8,128)(2,1)}), bf16[2,128,768]{2,1,0:T(8,128)(2,1)S(1)}, u32[]{:S(2)}, u32[]{:S(2)}) async-start(bf16[2,128,768]{2,1,0:T(8,128)(2,1)} %param.14), calls=%async_computation | async-start | bytes 786432 | tf_op jit(solution)/shard_map/all_to_all | solution.py:91
  43.7 17.9 %all-to-all-start.1 = ((f32[16,1,4608]{2,1,0:T(1,128)}), f32[16,1,4608]{2,1,0:T(1,128)S(1)}, u32[]{:S(2)}, u32[]{:S(2)}) async-start(f32[16,1,4608]{2,1,0:T(1,128)} %copy.61), calls=%async_computation.1 | async-start | bytes 589824 | tf_op jit(solution)/shard_map/all_to_all | solution.py:101
  61.7 10.5 %all-to-all-start.3 = ((bf16[2,128,768]{2,1,0:T(8,128)(2,1)}), bf16[2,128,768]{2,1,0:T(8,128)(2,1)S(1)}, u32[]{:S(2)}, u32[]{:S(2)}) async-start(bf16[2,128,768]{2,1,0:T(8,128)(2,1)} %param.16), calls=%async_computation.3 | async-start | bytes 786432 | tf_op jit(solution)/shard_map/all_to_all | solution.py:92
  65.5 280.9 %reduce-scatter.7.cloned.1.call-start = ((), (), s32[]{:S(2)}) async-start(), calls=%async_computation.15 | async-start | bytes 1216512 | tf_op jit(solution)/shard_map/reduce_scatter | solution.py:42
  212.8 7.1 copy-start.15
  219.8 1.8 copy-start.7
  219.8 2.4 copy-start.16
  219.9 4.0 copy-start.3
  223.9 3.9 copy-start.4
  227.1 0.7 copy-start.10
  229.3 4.8 copy-start.12
  234.1 1.9 copy-start.1
  239.5 2.5 copy-start.9
  239.5 2.5 copy-start.11
  250.7 152.7 %all-gather.16.cloned.1.call-start = ((), (), s32[]{:S(2)}) async-start(), calls=%async_computation.18 | async-start | bytes 1419264 | tf_op jit(solution)/shard_map/all_gather | solution.py:214
  250.7 3.1 copy-start.2
  254.8 256.3 %reduce-scatter.5.cloned.1.call-start = ((), (), s32[]{:S(2)}) async-start(), calls=%async_computation.14 | async-start | bytes 3649536 | tf_op jit(solution)/shard_map/reduce_scatter | solution.py:42
  258.0 1.4 copy-start.8
  258.1 364.9 %reduce-scatter.9.cloned.1.call-start = ((), (), s32[]{:S(2)}) async-start(), calls=%async_computation.16 | async-start | bytes 4866048 | tf_op jit(solution)/shard_map/reduce_scatter | solution.py:42
  263.2 1.0 copy-start.6
  263.2 472.2 %reduce-scatter.11.cloned.1.call-start = ((), (), s32[]{:S(2)}) async-start(), calls=%async_computation.17 | async-start | bytes 4866048 | tf_op jit(solution)/shard_map/reduce_scatter | solution.py:42
  270.5 1.0 copy-start.13
  270.5 9.4 %copy-start.5 = (f32[256,768]{1,0:T(8,128)S(1)}, f32[256,768]{1,0:T(8,128)}, u32[]{:S(2)}) copy-start(f32[256,768]{1,0:T(8,128)} %get-tuple-element.43) | copy-start | bytes 2359300
  276.5 10.7 %all-to-all-start.2 = ((bf16[2,2,49152]{2,1,0:T(2,128)(2,1)}), bf16[2,2,49152]{2,1,0:T(2,128)(2,1)S(1)}, u32[]{:S(2)}, u32[]{:S(2)}) async-start(bf16[2,2,49152]{2,1,0:T(2,128)(2,1)} %reshape.788), calls=%async_computation.2 | async-start | bytes 786432 | tf_op jit(solution)/shard_map/all_to_all | solution.py:148
  287.2 16.3 %all-to-all-start.4 = ((f32[1,256,768]{2,0,1:T(1,128)}), f32[1,256,768]{2,0,1:T(1,128)S(1)}, u32[]{:S(2)}, u32[]{:S(2)}) async-start(f32[1,256,768]{2,0,1:T(1,128)} %copy.70), calls=%async_computation.4 | async-start | bytes 1572864 | tf_op jit(solution)/shard_map/all_to_all | solution.py:200
  347.7 70.2 %copy-start.14 = (bf16[2,768]{1,0:T(2,128)(2,1)S(1)}, bf16[2,768]{1,0:T(2,128)(2,1)}, u32[]{:S(2)}) copy-start(bf16[2,768]{1,0:T(2,128)(2,1)} %param.15) | copy-start | bytes 9220
  405.7 11.0 %all-to-all-start.5 = ((f32[16,1,96]{2,1,0:T(1,128)}), f32[16,1,96]{2,1,0:T(1,128)S(1)}, u32[]{:S(2)}, u32[]{:S(2)}) async-start(f32[16,1,96]{2,1,0:T(1,128)} %bitcast.31), calls=%async_computation.5 | async-start | bytes 16384 | tf_op jit(solution)/shard_map/all_to_all | solution.py:238
Sparse Core Ops, SparseCore 0:
  10.3 55.0 all-gather.7
  67.7 36.8 all-gather.9
  106.9 51.9 all-gather.13
  161.1 51.6 all-gather.11
  250.8 95.5 reduce-scatter.6
  349.6 53.6 all-gather.15
  408.7 102.3 reduce-scatter.4
  516.6 106.3 reduce-scatter.8
  628.5 106.8 reduce-scatter.10
where the time goes:
time: 745 us; the launch traced here: 744 us
  waiting for transfers between devices  570 us (77%)
  matrix products  60.4 us (8%)
  local copies, waits for them, and re-layouts  29.6 us (4%)
  starting transfers between devices  23.8 us (3%)
  other arithmetic  23 us (3%)
  blocking collectives  22.7 us (3%)
  between operations  14.4 us (2%)
    reduce_scatter x4, waiting for transfers between devices, reduce_rows(): lax.psum_scatter(grad.astype(jnp.bfloat16), ('fsdp', 'sp'), scatter_dimen...  355 us
    all_gather x1, waiting for transfers between devices, body(): lax.all_gather(jnp.concatenate(grad_small), ('fsdp', 'sp'), axis=0)  55.6 us
    all_gather x1, waiting for transfers between devices, body(): down_full = lax.all_gather(w_down, 'fsdp', axis=0, tiled=True)  51.3 us
    all_gather x1, waiting for transfers between devices, body(): up_full = lax.all_gather(w_up, 'fsdp', axis=0, tiled=True)  48.3 us
    all_gather x1, blocking collectives, body(): lax.all_gather(jnp.concatenate(small).reshape(1, padded // 128, 128), 'fs...  22.7 us
    all_gather x1, waiting for transfers between devices, body(): out_full = lax.all_gather(w_out, 'fsdp', axis=0, tiled=True)  18.5 us
  transfers between devices with their start and end apart: 15, of which 13 were waited for; matrix products, arithmetic and copies ran while one was open for 9% of the time, Pallas kernels for 0%

commit v1 on v0

--- a/solution.py
+++ b/solution.py
@@ -7,6 +7,12 @@
 H = 12
 HD = 64
 eps = 1e-06
+
+
+def joined_along(pieces, dim):
+    pieces = jnp.moveaxis(pieces, 0, dim)
+    dims = pieces.shape
+    return pieces.reshape(*dims[:dim], dims[dim] * dims[dim + 1], *dims[dim + 2 :])
 
 
 def normalize(values):
@@ -112,7 +118,14 @@
     qkv_full = lax.all_gather(w_qkv, "fsdp", axis=0, tiled=True)
     out_full = lax.all_gather(w_out, "fsdp", axis=0, tiled=True)
     up_full = lax.all_gather(w_up, "fsdp", axis=0, tiled=True)
-    down_full = lax.all_gather(w_down, "fsdp", axis=0, tiled=True)
+    length = lax.axis_size("fsdp")
+    right = [(i, (i + 1) % length) for i in range(length)]
+    pieces_2 = [w_down]
+    while len(pieces_2) < length:
+        pieces_2.append(lax.ppermute(pieces_2[-1], "fsdp", right))
+    index = lax.axis_index("fsdp")
+    pieces_2 = jnp.stack(pieces_2)[(index - jnp.arange(length)) % length]
+    down_full = joined_along(pieces_2, 0)
     normed_one, inverse_one = normalize(inputs)
     attn_in = (normed_one * (1.0 + scale_one) + shift_one).astype(bf16)
     qkv_bias = jnp.concatenate([query_bias, jnp.zeros_like(query_bias), value_bias]).astype(f32)

time: 745 us -> 752 us (level)
  local copies, waits for them, and re-layouts: 29.6 us -> 47.4 us
  waiting for transfers between devices: 570 us -> 557 us
    ppermute x0 -> x15, waiting for transfers between devices: none -> 127 us  [body(): pieces_2.append(lax.ppermute(pieces_2[-1], 'fsdp', right))]
    all_gather x1 -> x0, waiting for transfers between devices: 51.3 us -> none  [body(): down_full = lax.all_gather(w_down, 'fsdp', axis=0, tiled=True)]
    all_gather x1, waiting for transfers between devices: 48.3 us -> 0.02 us  [body(): up_full = lax.all_gather(w_up, 'fsdp', axis=0, tiled=True)]
    all_gather x1, waiting for transfers between devices: 18.5 us -> 0.01 us  [body(): out_full = lax.all_gather(w_out, 'fsdp', axis=0, tiled=True)]
    all_to_all x1, waiting for transfers between devices: 13.6 us -> 0.01 us  [body(): lax.all_to_all(mod_part.reshape(fsdp_count, own_latents * 6 * D), 'fsdp',...]
    unnamed x52 -> x81, local copies, waits for them, and re-layouts: 12.9 us -> 23.6 us
  transfers between devices with their start and end apart: 15 -> 29, of which waited for: 13 -> 22; matrix products, arithmetic and copies ran while one was open for 9% -> 11% of each run, Pallas kernels for 0% -> 0%
where the time goes in v1:
time: 752 us; the launch traced here: 751 us
  waiting for transfers between devices  557 us (74%)
  matrix products  59.8 us (8%)
  local copies, waits for them, and re-layouts  47.4 us (6%)
  starting transfers between devices  26.1 us (3%)
  other arithmetic  23 us (3%)
  blocking collectives  22.8 us (3%)
  between operations  14.9 us (2%)
    reduce_scatter x4, waiting for transfers between devices, reduce_rows(): lax.psum_scatter(grad.astype(jnp.bfloat16), ('fsdp', 'sp'), scatter_dimen...  356 us
    ppermute x15, waiting for transfers between devices, body(): pieces_2.append(lax.ppermute(pieces_2[-1], 'fsdp', right))  127 us
    all_gather x1, waiting for transfers between devices, body(): lax.all_gather(jnp.concatenate(grad_small), ('fsdp', 'sp'), axis=0)  55.6 us
    unnamed x81, local copies, waits for them, and re-layouts  23.6 us
    all_gather x1, blocking collectives, body(): lax.all_gather(jnp.concatenate(small).reshape(1, padded // 128, 128), 'fs...  22.8 us
  transfers between devices with their start and end apart: 29, of which 22 were waited for; matrix products, arithmetic and copies ran while one was open for 11% of the time, Pallas kernels for 0%

profile of v1, /device:TPU:0, one launch (start us, length us, event | category | flops | bytes accessed | tf_op | source)
XLA Modules:
  0.0 751.1 jit_solution(12506185615900682669)
XLA Ops:
  8.7 4.2 all-to-all-start
  14.4 4.1 concatenate.17
  18.5 22.8 %all_gather.18 = bf16[16,32,128]{2,1,0:T(8,128)(2,1)S(1)} all-gather(bf16[1,32,128]{2,1,0:T(8,128)(2,1)S(1)} %bitcast.226), channel_id=1, replica_groups=mesh['fsdp'=16,'sp'=2] {'fsdp'}, dimensions={0}, use_global_device_ids=true | all-gather | bytes 139264 | tf_op jit(solution)/shard_map/all_gather | solution.py:86
  42.2 13.9 %collective-permute-done.1 = bf16[192,768]{1,0:T(8,128)(2,1)S(1)} collective-permute-done((bf16[192,768]{1,0:T(8,128)(2,1)S(1)}, bf16[192,768]{1,0:T(8,128)(2,1)S(1)}, u32[]{:S(2)}, u32[]{:S(2)}) %collective-permute-start.1) | collective-permute-done | bytes 294944 | tf_op jit(solution)/shard_map/ppermute | solution.py:125
  56.2 10.4 %collective-permute-done.2 = bf16[192,768]{1,0:T(8,128)(2,1)S(1)} collective-permute-done((bf16[192,768]{1,0:T(8,128)(2,1)S(1)}, bf16[192,768]{1,0:T(8,128)(2,1)S(1)}, u32[]{:S(2)}, u32[]{:S(2)}) %collective-permute-start.2) | collective-permute-done | bytes 294944 | tf_op jit(solution)/shard_map/ppermute | solution.py:125
  67.4 8.1 %collective-permute-done.3 = bf16[192,768]{1,0:T(8,128)(2,1)S(1)} collective-permute-done((bf16[192,768]{1,0:T(8,128)(2,1)S(1)}, bf16[192,768]{1,0:T(8,128)(2,1)S(1)}, u32[]{:S(2)}, u32[]{:S(2)}) %collective-permute-start.3) | collective-permute-done | bytes 294944 | tf_op jit(solution)/shard_map/ppermute | solution.py:125
  77.1 5.8 all-to-all-start.1
  83.1 2.5 collective-permute-done.4
  85.8 11.0 %collective-permute-done.5 = bf16[192,768]{1,0:T(8,128)(2,1)} collective-permute-done((bf16[192,768]{1,0:T(8,128)(2,1)S(1)}, bf16[192,768]{1,0:T(8,128)(2,1)}, u32[]{:S(2)}, u32[]{:S(2)}) %collective-permute-start.5) | collective-permute-done | bytes 294944 | tf_op jit(solution)/shard_map/ppermute | solution.py:125
  96.8 3.5 all-to-all-start.3
  101.3 5.9 collective-permute-done.6
  108.4 8.0 %collective-permute-done.7 = bf16[192,768]{1,0:T(8,128)(2,1)} collective-permute-done((bf16[192,768]{1,0:T(8,128)(2,1)}, bf16[192,768]{1,0:T(8,128)(2,1)}, u32[]{:S(2)}, u32[]{:S(2)}) %collective-permute-start.7) | collective-permute-done | bytes 294944 | tf_op jit(solution)/shard_map/ppermute | solution.py:125
  117.4 14.2 %collective-permute-done.8 = bf16[192,768]{1,0:T(8,128)(2,1)S(1)} collective-permute-done((bf16[192,768]{1,0:T(8,128)(2,1)}, bf16[192,768]{1,0:T(8,128)(2,1)S(1)}, u32[]{:S(2)}, u32[]{:S(2)}) %collective-permute-start.8) | collective-permute-done | bytes 294944 | tf_op jit(solution)/shard_map/ppermute | solution.py:125
  133.0 7.4 collective-permute-done.9
  141.2 1.7 bitcast_dynamic-update-slice_fusion.9
  142.9 12.8 %collective-permute-done.10 = bf16[192,768]{1,0:T(8,128)(2,1)S(1)} collective-permute-done((bf16[192,768]{1,0:T(8,128)(2,1)S(1)}, bf16[192,768]{1,0:T(8,128)(2,1)S(1)}, u32[]{:S(2)}, u32[]{:S(2)}) %collective-permute-start.10) | collective-permute-done | bytes 294944 | tf_op jit(solution)/shard_map/ppermute | solution.py:125
  155.7 1.7 bitcast_dynamic-update-slice_fusion.8
  157.4 1.7 bitcast_dynamic-update-slice_fusion.7
  159.1 11.0 %collective-permute-done.11 = bf16[192,768]{1,0:T(8,128)(2,1)S(1)} collective-permute-done((bf16[192,768]{1,0:T(8,128)(2,1)S(1)}, bf16[192,768]{1,0:T(8,128)(2,1)S(1)}, u32[]{:S(2)}, u32[]{:S(2)}) %collective-permute-start.11) | collective-permute-done | bytes 294944 | tf_op jit(solution)/shard_map/ppermute | solution.py:125
  171.6 7.4 collective-permute-done.12
  180.5 7.3 collective-permute-done.13
  189.3 7.4 collective-permute-done.14
  197.4 5.4 gather_fusion
  202.7 4.1 fusion.1
  206.8 1.6 copy.62
  208.4 2.2 fusion.55
  210.7 4.8 convolution_convert_fusion.4
  215.4 2.8 fusion.84
  218.5 4.0 convolution_add_fusion.1
  222.5 6.4 convert_reduce_fusion
  228.9 1.7 multiply_reduce_fusion.1
  230.7 3.3 fusion.21
  236.0 1.9 copy.66
  237.9 4.8 fusion.17
  242.7 1.8 fusion.54
  244.7 2.9 multiply_reduce_fusion
  248.2 1.4 fusion.19
  250.7 1.5 convolution_convert_fusion.3
  252.2 1.4 pad_maximum_fusion
  253.5 4.2 fusion.36
  257.7 1.7 convert.10
  259.5 3.0 multiply_reduce_fusion.2
  263.6 2.9 convolution_convert_fusion.2
  266.6 1.3 copy-done.8
  267.9 3.7 convolution_convert_fusion.1
  272.6 6.3 convolution_convert_fusion
  281.1 3.0 reduce.57
  284.9 3.5 all-to-all-start.2
  288.4 1.7 copy.70
  290.1 6.2 all-to-all-done.2
  296.3 3.5 all-to-all-start.4
  301.5 8.4 %all-to-all-done.4 = f32[1,256,768]{2,0,1:T(1,128)S(1)} async-done(((f32[1,256,768]{2,0,1:T(1,128)}), f32[1,256,768]{2,0,1:T(1,128)S(1)}, u32[]{:S(2)}, u32[]{:S(2)}) %all-to-all-start.4) | async-done | bytes 786464 | tf_op jit(solution)/shard_map/all_to_all | solution.py:213
  310.8 43.0 %reduce-scatter.7.cloned.1.call-done = bf16[24,768]{1,0:T(8,128)(2,1)} async-done(((bf16[768,768]{1,0:T(8,128)(2,1)}), bf16[24,768]{1,0:T(8,128)(2,1)}) %reduce-scatter.7.cloned.1.call-update) | async-done | bytes 36880 | tf_op jit(solution)/shard_map/reduce_scatter | solution.py:48
  353.9 1.4 convert_element_type.324
  355.3 55.6 %all-gather.13.cloned.1.call-done = f32[32,1,10752]{2,1,0:T(1,128)} async-done(((f32[1,1,10752]{2,1,0:T(1,128)}), f32[32,1,10752]{2,1,0:T(1,128)}) %all-gather.13.cloned.1.call-update) | async-done | bytes 1376272 | tf_op jit(solution)/shard_map/all_gather | solution.py:227
  410.9 1.4 copy.91
  413.2 4.6 all-to-all-start.5
  421.1 1.3 fusion.43
  426.2 92.3 %reduce-scatter.5.cloned.1.call-done = bf16[24,2304]{1,0:T(8,128)(2,1)} async-done(((bf16[768,2304]{1,0:T(8,128)(2,1)}), bf16[24,2304]{1,0:T(8,128)(2,1)}) %reduce-scatter.5.cloned.1.call-update) | async-done | bytes 110608 | tf_op jit(solution)/shard_map/reduce_scatter | solution.py:48
  518.5 1.6 convert_element_type.322
  520.1 110.5 %reduce-scatter.9.cloned.1.call-done = bf16[24,3072]{1,0:T(8,128)(2,1)} async-done(((bf16[768,3072]{1,0:T(8,128)(2,1)}), bf16[24,3072]{1,0:T(8,128)(2,1)}) %reduce-scatter.9.cloned.1.call-update) | async-done | bytes 147472 | tf_op jit(solution)/shard_map/reduce_scatter | solution.py:48
  630.6 1.6 convert_element_type.326
  632.2 110.3 %reduce-scatter.11.cloned.1.call-done = bf16[96,768]{1,0:T(8,128)(2,1)} async-done(((bf16[3072,768]{1,0:T(8,128)(2,1)}), bf16[96,768]{1,0:T(8,128)(2,1)}) %reduce-scatter.11.cloned.1.call-update) | async-done | bytes 147472 | tf_op jit(solution)/shard_map/reduce_scatter | solution.py:48
  742.6 1.6 convert_element_type.329
  (192 shorter events, 36.9 us)
Async XLA Ops:
  7.2 48.9 %copy-start = (bf16[48,4608]{1,0:T(8,128)(2,1)S(1)}, bf16[48,4608]{1,0:T(8,128)(2,1)}, u32[]{:S(2)}) copy-start(bf16[48,4608]{1,0:T(8,128)(2,1)} %param.17) | copy-start | bytes 1327108
  7.2 59.5 %copy-start.14 = (bf16[192,768]{1,0:T(8,128)(2,1)S(1)}, bf16[192,768]{1,0:T(8,128)(2,1)}, u32[]{:S(2)}) copy-start(bf16[192,768]{1,0:T(8,128)(2,1)} %param.26) | copy-start | bytes 884740
  7.2 195.5 %all-gather.7.cloned.1.call-start = ((), (), s32[]{:S(2)}) async-start(), calls=%async_computation.10 | async-start | bytes 3760128 | tf_op jit(solution)/shard_map/all_gather | solution.py:118
  7.9 207.5 %all-gather.9.cloned.1.call-start = ((), (), s32[]{:S(2)}) async-start(), calls=%async_computation.11 | async-start | bytes 1253376 | tf_op jit(solution)/shard_map/all_gather | solution.py:119
  8.7 68.4 %all-to-all-start = ((bf16[2,128,768]{2,1,0:T(8,128)(2,1)}), bf16[2,128,768]{2,1,0:T(8,128)(2,1)S(1)}, u32[]{:S(2)}, u32[]{:S(2)}) async-start(bf16[2,128,768]{2,1,0:T(8,128)(2,1)} %param.14), calls=%async_computation | async-start | bytes 786432 | tf_op jit(solution)/shard_map/all_to_all | solution.py:97
  12.9 205.5 %all-gather.11.cloned.1.call-start = ((), (), s32[]{:S(2)}) async-start(), calls=%async_computation.12 | async-start | bytes 5013504 | tf_op jit(solution)/shard_map/all_gather | solution.py:120
  12.9 28.8 %collective-permute-start = (bf16[192,768]{1,0:T(8,128)(2,1)}, bf16[192,768]{1,0:T(8,128)(2,1)S(1)}, u32[]{:S(2)}, u32[]{:S(2)}) collective-permute-start(bf16[192,768]{1,0:T(8,128)(2,1)} %param.26), channel_id=1, source_target_pairs={{0,2},{2,4},{4,6},{6,8},{8,10},{10,12},{12,14},{14,16},{16,18},{18... | collective-permute-start | bytes 884744 | tf_op jit(solution)/shard_map/ppermute | solution.py:125
  41.7 14.3 %collective-permute-start.1 = (bf16[192,768]{1,0:T(8,128)(2,1)S(1)}, bf16[192,768]{1,0:T(8,128)(2,1)S(1)}, u32[]{:S(2)}, u32[]{:S(2)}) collective-permute-start(bf16[192,768]{1,0:T(8,128)(2,1)S(1)} %collective-permute-done), channel_id=1, source_target_pairs={{0,2},{2,4},{4,6},{6,8},{8,10},{10,12},{12,14},{14,16},{16,18},{18... | collective-permute-start | bytes 884744 | tf_op jit(solution)/shard_map/ppermute | solution.py:125
  56.0 10.6 %collective-permute-start.2 = (bf16[192,768]{1,0:T(8,128)(2,1)S(1)}, bf16[192,768]{1,0:T(8,128)(2,1)S(1)}, u32[]{:S(2)}, u32[]{:S(2)}) collective-permute-start(bf16[192,768]{1,0:T(8,128)(2,1)S(1)} %collective-permute-done.1), channel_id=1, source_target_pairs={{0,2},{2,4},{4,6},{6,8},{8,10},{10,12},{12,14},{14,16},{16,18},{18... | collective-permute-start | bytes 884744 | tf_op jit(solution)/shard_map/ppermute | solution.py:125
  66.6 8.8 %collective-permute-start.3 = (bf16[192,768]{1,0:T(8,128)(2,1)S(1)}, bf16[192,768]{1,0:T(8,128)(2,1)S(1)}, u32[]{:S(2)}, u32[]{:S(2)}) collective-permute-start(bf16[192,768]{1,0:T(8,128)(2,1)S(1)} %collective-permute-done.2), channel_id=1, source_target_pairs={{0,2},{2,4},{4,6},{6,8},{8,10},{10,12},{12,14},{14,16},{16,18},{18... | collective-permute-start | bytes 884744 | tf_op jit(solution)/shard_map/ppermute | solution.py:125
  75.5 31.8 %copy-start.15 = (bf16[192,768]{1,0:T(8,128)(2,1)}, bf16[192,768]{1,0:T(8,128)(2,1)S(1)}, u32[]{:S(2)}) copy-start(bf16[192,768]{1,0:T(8,128)(2,1)S(1)} %collective-permute-done.3) | copy-start | bytes 884740
  75.5 10.1 %collective-permute-start.4 = (bf16[192,768]{1,0:T(8,128)(2,1)S(1)}, bf16[192,768]{1,0:T(8,128)(2,1)S(1)}, u32[]{:S(2)}, u32[]{:S(2)}) collective-permute-start(bf16[192,768]{1,0:T(8,128)(2,1)S(1)} %collective-permute-done.3), channel_id=1, source_target_pairs={{0,2},{2,4},{4,6},{6,8},{8,10},{10,12},{12,14},{14,16},{16,18},{18... | collective-permute-start | bytes 884744 | tf_op jit(solution)/shard_map/ppermute | solution.py:125
  77.1 19.7 %all-to-all-start.1 = ((f32[16,1,4608]{2,1,0:T(1,128)}), f32[16,1,4608]{2,1,0:T(1,128)S(1)}, u32[]{:S(2)}, u32[]{:S(2)}) async-start(f32[16,1,4608]{2,1,0:T(1,128)} %copy.61), calls=%async_computation.1 | async-start | bytes 589824 | tf_op jit(solution)/shard_map/all_to_all | solution.py:107
  85.6 11.2 %collective-permute-start.5 = (bf16[192,768]{1,0:T(8,128)(2,1)S(1)}, bf16[192,768]{1,0:T(8,128)(2,1)}, u32[]{:S(2)}, u32[]{:S(2)}) collective-permute-start(bf16[192,768]{1,0:T(8,128)(2,1)S(1)} %collective-permute-done.4), channel_id=1, source_target_pairs={{0,2},{2,4},{4,6},{6,8},{8,10},{10,12},{12,14},{14,16},{16,18},{18... | collective-permute-start | bytes 884744 | tf_op jit(solution)/shard_map/ppermute | solution.py:125
  96.8 10.4 %collective-permute-start.6 = (bf16[192,768]{1,0:T(8,128)(2,1)}, bf16[192,768]{1,0:T(8,128)(2,1)}, u32[]{:S(2)}, u32[]{:S(2)}) collective-permute-start(bf16[192,768]{1,0:T(8,128)(2,1)} %collective-permute-done.5), channel_id=1, source_target_pairs={{0,2},{2,4},{4,6},{6,8},{8,10},{10,12},{12,14},{14,16},{16,18},{18... | collective-permute-start | bytes 884744 | tf_op jit(solution)/shard_map/ppermute | solution.py:125
  96.8 10.5 %all-to-all-start.3 = ((bf16[2,128,768]{2,1,0:T(8,128)(2,1)}), bf16[2,128,768]{2,1,0:T(8,128)(2,1)S(1)}, u32[]{:S(2)}, u32[]{:S(2)}) async-start(bf16[2,128,768]{2,1,0:T(8,128)(2,1)} %param.16), calls=%async_computation.3 | async-start | bytes 786432 | tf_op jit(solution)/shard_map/all_to_all | solution.py:98
  100.3 253.6 %reduce-scatter.7.cloned.1.call-start = ((), (), s32[]{:S(2)}) async-start(), calls=%async_computation.14 | async-start | bytes 1216512 | tf_op jit(solution)/shard_map/reduce_scatter | solution.py:48
  107.2 9.2 %collective-permute-start.7 = (bf16[192,768]{1,0:T(8,128)(2,1)}, bf16[192,768]{1,0:T(8,128)(2,1)}, u32[]{:S(2)}, u32[]{:S(2)}) collective-permute-start(bf16[192,768]{1,0:T(8,128)(2,1)} %collective-permute-done.6), channel_id=1, source_target_pairs={{0,2},{2,4},{4,6},{6,8},{8,10},{10,12},{12,14},{14,16},{16,18},{18... | collective-permute-start | bytes 884744 | tf_op jit(solution)/shard_map/ppermute | solution.py:125
  107.3 51.8 %copy-start.5 = (bf16[2,128,768]{2,1,0:T(8,128)(2,1)}, bf16[2,128,768]{2,1,0:T(8,128)(2,1)S(1)}, u32[]{:S(2)}) copy-start(bf16[2,128,768]{2,1,0:T(8,128)(2,1)S(1)} %all-to-all-done.3) | copy-start | bytes 1179652
  107.3 25.0 %copy-start.16 = (bf16[192,768]{1,0:T(8,128)(2,1)S(1)}, bf16[192,768]{1,0:T(8,128)(2,1)}, u32[]{:S(2)}) copy-start(bf16[192,768]{1,0:T(8,128)(2,1)} %copy-done.15) | copy-start | bytes 884740
  116.4 15.2 %collective-permute-start.8 = (bf16[192,768]{1,0:T(8,128)(2,1)}, bf16[192,768]{1,0:T(8,128)(2,1)S(1)}, u32[]{:S(2)}, u32[]{:S(2)}) collective-permute-start(bf16[192,768]{1,0:T(8,128)(2,1)} %collective-permute-done.7), channel_id=1, source_target_pairs={{0,2},{2,4},{4,6},{6,8},{8,10},{10,12},{12,14},{14,16},{16,18},{18... | collective-permute-start | bytes 884744 | tf_op jit(solution)/shard_map/ppermute | solution.py:125
  131.6 8.8 %collective-permute-start.9 = (bf16[192,768]{1,0:T(8,128)(2,1)S(1)}, bf16[192,768]{1,0:T(8,128)(2,1)S(1)}, u32[]{:S(2)}, u32[]{:S(2)}) collective-permute-start(bf16[192,768]{1,0:T(8,128)(2,1)S(1)} %collective-permute-done.8), channel_id=1, source_target_pairs={{0,2},{2,4},{4,6},{6,8},{8,10},{10,12},{12,14},{14,16},{16,18},{18... | collective-permute-start | bytes 884744 | tf_op jit(solution)/shard_map/ppermute | solution.py:125
  140.4 15.3 %collective-permute-start.10 = (bf16[192,768]{1,0:T(8,128)(2,1)S(1)}, bf16[192,768]{1,0:T(8,128)(2,1)S(1)}, u32[]{:S(2)}, u32[]{:S(2)}) collective-permute-start(bf16[192,768]{1,0:T(8,128)(2,1)S(1)} %collective-permute-done.9), channel_id=1, source_target_pairs={{0,2},{2,4},{4,6},{6,8},{8,10},{10,12},{12,14},{14,16},{16,18},{18... | collective-permute-start | bytes 884744 | tf_op jit(solution)/shard_map/ppermute | solution.py:125
  155.7 14.4 %collective-permute-start.11 = (bf16[192,768]{1,0:T(8,128)(2,1)S(1)}, bf16[192,768]{1,0:T(8,128)(2,1)S(1)}, u32[]{:S(2)}, u32[]{:S(2)}) collective-permute-start(bf16[192,768]{1,0:T(8,128)(2,1)S(1)} %collective-permute-done.10), channel_id=1, source_target_pairs={{0,2},{2,4},{4,6},{6,8},{8,10},{10,12},{12,14},{14,16},{16,18},{18... | collective-permute-start | bytes 884744 | tf_op jit(solution)/shard_map/ppermute | solution.py:125
  170.1 8.8 %collective-permute-start.12 = (bf16[192,768]{1,0:T(8,128)(2,1)S(1)}, bf16[192,768]{1,0:T(8,128)(2,1)S(1)}, u32[]{:S(2)}, u32[]{:S(2)}) collective-permute-start(bf16[192,768]{1,0:T(8,128)(2,1)S(1)} %collective-permute-done.11), channel_id=1, source_target_pairs={{0,2},{2,4},{4,6},{6,8},{8,10},{10,12},{12,14},{14,16},{16,18},{18... | collective-permute-start | bytes 884744 | tf_op jit(solution)/shard_map/ppermute | solution.py:125
  179.0 8.8 %collective-permute-start.13 = (bf16[192,768]{1,0:T(8,128)(2,1)S(1)}, bf16[192,768]{1,0:T(8,128)(2,1)S(1)}, u32[]{:S(2)}, u32[]{:S(2)}) collective-permute-start(bf16[192,768]{1,0:T(8,128)(2,1)S(1)} %collective-permute-done.12), channel_id=1, source_target_pairs={{0,2},{2,4},{4,6},{6,8},{8,10},{10,12},{12,14},{14,16},{16,18},{18... | collective-permute-start | bytes 884744 | tf_op jit(solution)/shard_map/ppermute | solution.py:125
  187.8 8.8 %collective-permute-start.14 = (bf16[192,768]{1,0:T(8,128)(2,1)S(1)}, bf16[192,768]{1,0:T(8,128)(2,1)S(1)}, u32[]{:S(2)}, u32[]{:S(2)}) collective-permute-start(bf16[192,768]{1,0:T(8,128)(2,1)S(1)} %collective-permute-done.13), channel_id=1, source_target_pairs={{0,2},{2,4},{4,6},{6,8},{8,10},{10,12},{12,14},{14,16},{16,18},{18... | collective-permute-start | bytes 884744 | tf_op jit(solution)/shard_map/ppermute | solution.py:125
  218.5 4.0 copy-start.13
  218.5 10.4 %slice-start.2 = ((s8[4718592]{0:T(1024)(128)(4,1)}), s8[4194304]{0:T(1024)(128)(4,1)S(1)}, s32[]{:S(2)}) async-start(s8[4718592]{0:T(1024)(128)(4,1)} %bitcast.228), calls=%async_computation.20 | async-start | bytes 8388608
  218.5 12.1 %slice-start = ((s8[4718592]{0:T(1024)(128)(4,1)}), s8[4194304]{0:T(1024)(128)(4,1)S(1)}, s32[]{:S(2)}) async-start(s8[4718592]{0:T(1024)(128)(4,1)} %bitcast.204), calls=%async_computation.18 | async-start | bytes 8388608
  222.5 8.2 %copy-start.18 = (f32[256,3072]{1,0:T(8,128)}, f32[256,3072]{1,0:T(8,128)S(1)}, u32[]{:S(2)}) copy-start(f32[256,3072]{1,0:T(8,128)S(1)} %convolution_add_fusion.1) | copy-start | bytes 9437188
  222.5 6.4 slice-start.3
  222.5 8.2 %slice-start.1 = ((s8[4718592]{0:T(1024)(128)(4,1)}), s8[524288]{0:T(1024)(128)(4,1)S(1)}, s32[]{:S(2)}) async-start(s8[4718592]{0:T(1024)(128)(4,1)} %bitcast.204), calls=%async_computation.19 | async-start | bytes 1048576
  228.9 1.7 copy-start.7
  228.9 1.8 copy-start.6
  230.7 4.1 copy-start.3
  234.0 0.7 copy-start.10
  242.7 2.0 copy-start.1
  248.2 2.5 copy-start.9
  248.2 2.5 copy-start.11
  259.4 151.5 %all-gather.13.cloned.1.call-start = ((), (), s32[]{:S(2)}) async-start(), calls=%async_computation.17 | async-start | bytes 1419264 | tf_op jit(solution)/shard_map/all_gather | solution.py:227
  259.5 3.1 copy-start.2
  263.6 255.0 %reduce-scatter.5.cloned.1.call-start = ((), (), s32[]{:S(2)}) async-start(), calls=%async_computation.13 | async-start | bytes 3649536 | tf_op jit(solution)/shard_map/reduce_scatter | solution.py:48
  266.5 1.4 copy-start.8
  266.5 364.0 %reduce-scatter.9.cloned.1.call-start = ((), (), s32[]{:S(2)}) async-start(), calls=%async_computation.15 | async-start | bytes 4866048 | tf_op jit(solution)/shard_map/reduce_scatter | solution.py:48
  271.6 1.0 copy-start.19
  271.6 470.9 %reduce-scatter.11.cloned.1.call-start = ((), (), s32[]{:S(2)}) async-start(), calls=%async_computation.16 | async-start | bytes 4866048 | tf_op jit(solution)/shard_map/reduce_scatter | solution.py:48
  278.9 1.0 copy-start.12
  279.0 9.4 %copy-start.4 = (f32[256,768]{1,0:T(8,128)S(1)}, f32[256,768]{1,0:T(8,128)}, u32[]{:S(2)}) copy-start(f32[256,768]{1,0:T(8,128)} %get-tuple-element.45) | copy-start | bytes 2359300
  284.9 11.4 %all-to-all-start.2 = ((bf16[2,2,49152]{2,1,0:T(2,128)(2,1)}), bf16[2,2,49152]{2,1,0:T(2,128)(2,1)S(1)}, u32[]{:S(2)}, u32[]{:S(2)}) async-start(bf16[2,2,49152]{2,1,0:T(2,128)(2,1)} %reshape.854), calls=%async_computation.2 | async-start | bytes 786432 | tf_op jit(solution)/shard_map/all_to_all | solution.py:161
  296.3 13.6 %all-to-all-start.4 = ((f32[1,256,768]{2,0,1:T(1,128)}), f32[1,256,768]{2,0,1:T(1,128)S(1)}, u32[]{:S(2)}, u32[]{:S(2)}) async-start(f32[1,256,768]{2,0,1:T(1,128)} %copy.70), calls=%async_computation.4 | async-start | bytes 1572864 | tf_op jit(solution)/shard_map/all_to_all | solution.py:213
  355.3 70.2 %copy-start.17 = (bf16[2,768]{1,0:T(2,128)(2,1)S(1)}, bf16[2,768]{1,0:T(2,128)(2,1)}, u32[]{:S(2)}) copy-start(bf16[2,768]{1,0:T(2,128)(2,1)} %param.15) | copy-start | bytes 9220
  413.2 11.0 %all-to-all-start.5 = ((f32[16,1,96]{2,1,0:T(1,128)}), f32[16,1,96]{2,1,0:T(1,128)S(1)}, u32[]{:S(2)}, u32[]{:S(2)}) async-start(f32[16,1,96]{2,1,0:T(1,128)} %bitcast.50), calls=%async_computation.5 | async-start | bytes 16384 | tf_op jit(solution)/shard_map/all_to_all | solution.py:251
Sparse Core Ops, SparseCore 0:
  10.3 52.3 all-gather.6
  65.0 42.3 all-gather.8
  109.7 57.5 all-gather.10
  259.5 94.3 reduce-scatter.6
  357.2 53.6 all-gather.12
  416.1 102.3 reduce-scatter.4
  524.0 106.5 reduce-scatter.8
  636.1 106.4 reduce-scatter.10
